TPU v7x, 256 devices: a whole 4x4x8 slice. The times are simulated.
256 devices in a mesh: win: 8 (over x, core), obs: 32 (over y, z).
Axes of the slice: x: 4, y: 4, z: 8, core: 2. Of those that a mesh axis runs over, the one named last changes fastest.
Arguments:
- predictors: float32 [8, 8, 1048576], P('win', None, 'obs'), may hold values from -8 to 8
- departures: float32 [8, 1048576], P('win', 'obs'), may hold values from -30 to 30
- channel: int32 [8, 1048576], P('win', 'obs'), may hold values from 0 to 299
- decay_rate: float32 [8, 300], P('win'), may hold values from 0.5 to 1
- ridge_counts: int32 [8, 300], P('win'), may hold values from 874 to 3496
Outputs:
- coefficients: float32 [8, 8, 300], P('win')
- corrected: float32 [8, 1048576], P('win', 'obs')
All inputs are finite; a program needn't handle non-finite values.
Results may differ from a plain program's by a relative error of at most 0.00013.
Values sent between devices are 32-bit elements; how exact they have to be, the bound alone decides.
No kernel may reach another device: no remote copies, remote signals or barrier semaphores. Data moves between devices by JAX's collectives and lax.ppermute only.
A program may use at most 64 MiB of HBM per device.

v0:
```python
import functools

import jax
import jax.numpy as jnp
from jax import lax
from jax.experimental import pallas as pl
from jax.experimental.pallas import tpu as pltpu
from jax.sharding import PartitionSpec as P

ROUNDS = 3
EDGE = 1.5

LANES = 128
SUB = 8
OWNERS = 32
SLOTS = 10
HALF = 5
SPLIT = HALF * OWNERS
FEATS = 48
CHUNK = 1024


def channel_row(ref):
    count = ref.shape[1]
    rows = []
    for start in range(0, 3 * LANES, LANES):
        stop = min(start + LANES, count)
        row = ref[:, start:stop].astype(jnp.float32)
        if stop - start < LANES:
            fill = jnp.ones((1, LANES - (stop - start)), jnp.float32)
            row = jnp.concatenate([row, fill], axis=1)
        rows.append(row)
    return rows


def pick(tables, index):
    low = index & (LANES - 1)
    high = index >> 7
    first, second, third = [jnp.take_along_axis(t, low, axis=1) for t in tables]
    return jnp.where(high == 0, first, jnp.where(high == 1, second, third))


def build_tables(got_ref):
    square = jnp.concatenate(
        [got_ref[...], jnp.zeros((LANES - OWNERS, LANES), jnp.float32)], axis=0
    ).T
    lane = lax.broadcasted_iota(jnp.int32, (SUB, LANES), 1)
    tables = []
    for t in range(3):
        table = jnp.zeros((SUB, LANES), jnp.float32)
        for q in range(4):
            slot = 4 * t + q
            if slot >= SLOTS:
                continue
            tile = square[slot * SUB : (slot + 1) * SUB, :]
            if q:
                tile = pltpu.roll(tile, q * OWNERS, 1)
            table = jnp.where((lane >> 5) == q, tile, table)
        tables.append(table)
    return tables


def fit(predictors, channels, tables):
    parts = []
    for g in range(predictors.shape[1] // LANES):
        at = slice(g * LANES, (g + 1) * LANES)
        index = jnp.broadcast_to(channels[:, at], (SUB, LANES))
        parts.append(predictors[:, at] * pick(tables, index))
    return jnp.sum(jnp.concatenate(parts, axis=1), axis=0, keepdims=True)


def statistics_kernel(first, *refs):
    if first:
        pred_ref, dep_ref, chan_ref, out_ref, acc_ref = refs
    else:
        pred_ref, dep_ref, chan_ref, got_ref, out_ref, acc_ref = refs
        tables = build_tables(got_ref)
    total = pred_ref.shape[1]
    acc_ref[...] = jnp.zeros_like(acc_ref)
    row_id = lax.broadcasted_iota(jnp.int32, (SPLIT, CHUNK), 0)

    def step(i, carry):
        at = pl.ds(pl.multiple_of(i * CHUNK, CHUNK), CHUNK)
        p = pred_ref[:, at]
        d = dep_ref[:, at]
        c = chan_ref[:, at]
        residual = d if first else d - fit(p, c, tables)
        weight = EDGE / jnp.maximum(jnp.abs(residual), EDGE)
        wp = p * weight
        rows = [wp * p]
        for offset in range(1, 5):
            rows.append(wp * pltpu.roll(p, SUB - offset, 0))
        rows.append(wp * d)
        feats = jnp.concatenate(rows, axis=0)
        head = feats.astype(jnp.bfloat16)
        tail = (feats - head.astype(jnp.float32)).astype(jnp.bfloat16)
        upper = c >= SPLIT
        in_upper = upper.astype(jnp.float32).astype(jnp.bfloat16)
        in_lower = 1.0 - in_upper
        columns = jnp.concatenate(
            [head * in_lower, head * in_upper, tail * in_lower, tail * in_upper], axis=0
        )
        local = jnp.where(upper, c - SPLIT, c)
        hot = (row_id == local).astype(jnp.float32).astype(jnp.bfloat16)
        acc_ref[...] += lax.dot_general(
            hot, columns, (((1,), (1,)), ((), ())), preferred_element_type=jnp.float32
        )
        return carry

    lax.fori_loop(0, total // CHUNK, step, 0)
    wide = 2 * FEATS
    sums = acc_ref[:, :wide] + acc_ref[:, wide:]
    sums = jnp.concatenate([sums, jnp.zeros((SPLIT, LANES - wide), jnp.float32)], axis=1)
    last = sums[4 * OWNERS :, :]
    lane = lax.broadcasted_iota(jnp.int32, (OWNERS, LANES), 1)
    for j in range(4):
        rows = sums[j * OWNERS : (j + 1) * OWNERS, :]
        if j < 3:
            rows = jnp.where(lane < wide, rows, pltpu.roll(last, wide - 32 * j, 1))
        out_ref[pl.ds(j, OWNERS, stride=4), :] = rows


def packed_slots():
    row = lax.broadcasted_iota(jnp.int32, (SUB, LANES), 0)
    lane = lax.broadcasted_iota(jnp.int32, (SUB, LANES), 1)
    row = row & 3
    wide = 2 * FEATS
    spilled = lane >= wide
    column = jnp.where(spilled, 32 * row + lane - wide, lane)
    j = jnp.where(spilled, 4, row)
    return jnp.where(column >= FEATS, HALF, 0) + j


def reduce_kernel(parts_ref, decay_ref, out_ref):
    owner = lax.axis_index("obs")
    summed = parts_ref[0:SUB, :]
    for t in range(1, parts_ref.shape[0] // SUB):
        summed = summed + parts_ref[t * SUB : (t + 1) * SUB, :]
    summed = summed + pltpu.roll(summed, 4, 0)
    index = jnp.minimum(packed_slots(), SLOTS - 1) * OWNERS + owner
    tables = [jnp.broadcast_to(r, (SUB, LANES)) for r in channel_row(decay_ref)]
    decay = pick(tables, index)
    row = lax.broadcasted_iota(jnp.int32, (SUB, LANES), 0)
    tile = jnp.where(row < 4, summed, decay)
    for t in range(out_ref.shape[0] // SUB):
        out_ref[t * SUB : (t + 1) * SUB, :] = tile


def solve_kernel(all_ref, ridge_ref, out_ref):
    owner = lax.axis_index("obs")
    window = lax.axis_index("win")
    row = lax.broadcasted_iota(jnp.int32, (SUB, LANES), 0)
    lane = lax.broadcasted_iota(jnp.int32, (SUB, LANES), 1)
    wide = 2 * FEATS

    carried = jnp.zeros((SUB, LANES), jnp.float32)
    kept = carried
    for w in range(all_ref.shape[0] // SUB):
        tile = all_ref[w * SUB : (w + 1) * SUB, :]
        carried = pltpu.roll(tile, 4, 0) * carried + tile
        kept = jnp.where(window == w, carried, kept)

    spilled = [
        pltpu.roll(pltpu.roll(kept, (32 * j + LANES - wide) % LANES, 1), 4 - j, 0)
        for j in range(3)
    ]
    fifth = jnp.where(lane < 32, spilled[0], jnp.where(lane < 64, spilled[1], spilled[2]))
    tile = jnp.where(row < 4, kept, jnp.where(row == 4, fifth, 0.0))
    square = jnp.concatenate(
        [tile, jnp.zeros((LANES - SUB, LANES), jnp.float32)], axis=0
    ).T
    blocks = []
    for b in range(6):
        low = square[b * SUB : (b + 1) * SUB, :]
        high = square[FEATS + b * SUB : FEATS + (b + 1) * SUB, :]
        blocks.append(jnp.where(lane < HALF, low, pltpu.roll(high, HALF, 1)))

    index = jnp.minimum(lane, SLOTS - 1) * OWNERS + owner
    ridge = pick([jnp.broadcast_to(r, (SUB, LANES)) for r in channel_row(ridge_ref)], index)

    offsets = blocks[:5]
    for d in range(5, SUB):
        offsets.append(pltpu.roll(blocks[SUB - d], SUB - d, 0))
    offsets[0] = offsets[0] + ridge
    columns = []
    for j in range(SUB):
        column = offsets[0]
        for d in range(1, SUB):
            column = jnp.where(row == (j - d) % SUB, offsets[d], column)
        columns.append(column)

    def spread(x, i):
        return jnp.broadcast_to(x[i : i + 1, :], (SUB, LANES))

    right = blocks[5]
    inverse = jnp.ones((SUB, LANES), jnp.float32)
    for j in range(SUB):
        inv = 1.0 / spread(columns[j], j)
        inverse = jnp.where(row == j, inv, inverse)
        factor = jnp.where(row > j, columns[j] * inv, 0.0)
        for k in range(j + 1, SUB):
            columns[k] = columns[k] - factor * spread(columns[k], j)
        right = right - factor * spread(right, j)
    answer = right * inverse
    for j in range(SUB - 1, 0, -1):
        factor = jnp.where(row < j, columns[j] * inverse, 0.0)
        answer = answer - factor * spread(answer, j)

    flat = jnp.take_along_axis(answer, lane >> 3, axis=1)
    flat = jnp.sum(jnp.where(row == (lane & 7), flat, 0.0), axis=0, keepdims=True)
    out_ref[...] = jnp.broadcast_to(flat, out_ref.shape)


def correct_kernel(pred_ref, dep_ref, chan_ref, got_ref, coef_ref, out_ref):
    tables = build_tables(got_ref)
    count = coef_ref.shape[1]
    for t in range(3):
        stop = min((t + 1) * LANES, count)
        coef_ref[:, t * LANES : stop] = tables[t][:, : stop - t * LANES]

    def step(i, carry):
        at = pl.ds(pl.multiple_of(i * CHUNK, CHUNK), CHUNK)
        out_ref[:, at] = dep_ref[:, at] - fit(pred_ref[:, at], chan_ref[:, at], tables)
        return carry

    lax.fori_loop(0, pred_ref.shape[1] // CHUNK, step, 0)


def call(kernel, name, out_shape, operands, scratch=()):
    vmem = pl.BlockSpec(memory_space=pltpu.VMEM)
    several = isinstance(out_shape, list)
    return pl.pallas_call(
        kernel,
        name=name,
        out_shape=out_shape,
        in_specs=[vmem] * len(operands),
        out_specs=[vmem] * len(out_shape) if several else vmem,
        scratch_shapes=list(scratch),
        compiler_params=pltpu.CompilerParams(vmem_limit_bytes=32 << 20),
    )(*operands)


def shape(*dims):
    return jax.ShapeDtypeStruct(dims, jnp.float32)


def body(predictors, departures, channel, decay_rate, ridge_counts):
    channels = decay_rate.shape[1]
    total = departures.shape[1]
    rows_here = predictors[0]
    windows = lax.axis_size("win")
    got = None
    for _ in range(ROUNDS):
        operands = [rows_here, departures, channel] + ([] if got is None else [got])
        parts = call(
            functools.partial(statistics_kernel, got is None),
            "statistics",
            shape(4 * OWNERS, LANES),
            operands,
            [pltpu.VMEM((SPLIT, 4 * FEATS), jnp.float32)],
        )
        parts = lax.all_to_all(parts, "obs", 0, 0, tiled=True)
        tile = call(reduce_kernel, "reduce", shape(windows * SUB, LANES), [parts, decay_rate])
        tiles = lax.all_to_all(tile, "win", 0, 0, tiled=True)
        flat = call(solve_kernel, "solve", shape(OWNERS, LANES), [tiles, ridge_counts])
        got = lax.all_to_all(flat, "obs", 0, 0, tiled=True)
    coeffs, corrected = call(
        correct_kernel,
        "correct",
        [shape(SUB, channels), shape(1, total)],
        [rows_here, departures, channel, got],
    )
    return (coeffs[None], corrected)


def solution(mesh):
    placed = (
        P("win", None, "obs"),
        P("win", "obs"),
        P("win", "obs"),
        P("win", None),
        P("win", None),
    )
    return jax.shard_map(
        body,
        mesh=mesh,
        in_specs=placed,
        out_specs=(P("win", None, None), P("win", "obs")),
        check_vma=False,
    )
```

profile of v0, /device:TPU:1, one launch (start us, length us, event | category | flops | bytes accessed | tf_op | source)
XLA Modules:
  0.0 160.8 jit_solution(16229032821716326822)
XLA Ops:
  0.6 0.0 copy-start
  0.6 1.2 copy-done
  1.9 0.0 copy-start.2
  1.9 0.9 copy-done.2
  2.8 0.0 copy-start.3
  2.8 0.9 copy-done.3
  3.7 0.0 copy-start.1
  3.7 9.7 %statistics.3 = f32[128,128]{1,0:T(8,128)S(1)} custom-call(f32[8,32768]{1,0:T(8,128)S(1)} %bitcast.26, f32[1,32768]{1,0:T(1,128)S(1)} %copy-done.2, s32[1,32768]{1,0:T(1,128)S(1)} %copy-done.3), custom_call_target="tpu_custom_call" | custom-call | tf_op jit(solution)/shard_map/statistics/pallas_call | solution.py:232
  13.4 20.7 %all_to_all.99 = f32[32,4,128]{2,1,0:T(4,128)S(1)} all-to-all(f32[32,4,128]{2,1,0:T(4,128)S(1)} %bitcast.35), channel_id=1, replica_groups=mesh['win'=8,'obs'=32] {'obs'}, dimensions={0} | all-to-all | bytes 131072 | tf_op jit(solution)/shard_map/all_to_all | solution.py:262
  34.1 0.0 copy-start.5
  34.1 0.7 copy-done.5
  34.7 0.1 reduce.3
  34.8 10.9 %all_to_all.100 = f32[8,8,128]{2,1,0:T(8,128)S(1)} all-to-all(f32[8,8,128]{2,1,0:T(8,128)S(1)} %bitcast.36), channel_id=1, replica_groups=mesh['win'=8,'obs'=32] {'win'}, dimensions={0} | all-to-all | bytes 65536 | tf_op jit(solution)/shard_map/all_to_all | solution.py:264
  45.7 0.0 copy-start.4
  45.7 0.7 copy-done.4
  46.4 0.4 solve.3
  46.8 11.6 %all_to_all.101 = f32[32,1,128]{2,1,0:T(1,128)S(1)} all-to-all(f32[32,1,128]{2,1,0:T(1,128)S(1)} %bitcast.44), channel_id=1, replica_groups=mesh['win'=8,'obs'=32] {'obs'}, dimensions={0} | all-to-all | bytes 32768 | tf_op jit(solution)/shard_map/all_to_all | solution.py:266
  58.5 0.0 copy-done.1
  58.5 14.3 %statistics.4 = f32[128,128]{1,0:T(8,128)S(1)} custom-call(f32[8,32768]{1,0:T(8,128)S(1)} %bitcast.27, f32[1,32768]{1,0:T(1,128)S(1)} %copy-done.2, s32[1,32768]{1,0:T(1,128)S(1)} %copy-done.3, f32[32,128]{1,0:T(8,128)S(1)} %bitcast.42), custom_call_target="tpu_custom_call" | custom-call | tf_op jit(solution)/shard_map/statistics/pallas_call | solution.py:232
  72.8 11.8 %all_to_all.102 = f32[32,4,128]{2,1,0:T(4,128)S(1)} all-to-all(f32[32,4,128]{2,1,0:T(4,128)S(1)} %bitcast.30), channel_id=1, replica_groups=mesh['win'=8,'obs'=32] {'obs'}, dimensions={0} | all-to-all | bytes 131072 | tf_op jit(solution)/shard_map/all_to_all | solution.py:262
  84.6 0.1 reduce.4
  84.7 10.3 %all_to_all.103 = f32[8,8,128]{2,1,0:T(8,128)S(1)} all-to-all(f32[8,8,128]{2,1,0:T(8,128)S(1)} %bitcast.37), channel_id=1, replica_groups=mesh['win'=8,'obs'=32] {'win'}, dimensions={0} | all-to-all | bytes 65536 | tf_op jit(solution)/shard_map/all_to_all | solution.py:264
  95.0 0.4 solve.4
  95.4 11.6 %all_to_all.104 = f32[32,1,128]{2,1,0:T(1,128)S(1)} all-to-all(f32[32,1,128]{2,1,0:T(1,128)S(1)} %bitcast.45), channel_id=1, replica_groups=mesh['win'=8,'obs'=32] {'obs'}, dimensions={0} | all-to-all | bytes 32768 | tf_op jit(solution)/shard_map/all_to_all | solution.py:266
  107.0 14.3 %statistics.5 = f32[128,128]{1,0:T(8,128)S(1)} custom-call(f32[8,32768]{1,0:T(8,128)S(1)} %bitcast.28, f32[1,32768]{1,0:T(1,128)S(1)} %copy-done.2, s32[1,32768]{1,0:T(1,128)S(1)} %copy-done.3, f32[32,128]{1,0:T(8,128)S(1)} %bitcast.43), custom_call_target="tpu_custom_call" | custom-call | tf_op jit(solution)/shard_map/statistics/pallas_call | solution.py:232
  121.3 11.8 %all_to_all.105 = f32[32,4,128]{2,1,0:T(4,128)S(1)} all-to-all(f32[32,4,128]{2,1,0:T(4,128)S(1)} %bitcast.31), channel_id=1, replica_groups=mesh['win'=8,'obs'=32] {'obs'}, dimensions={0} | all-to-all | bytes 131072 | tf_op jit(solution)/shard_map/all_to_all | solution.py:262
  133.1 0.1 reduce.5
  133.2 10.3 %all_to_all.106 = f32[8,8,128]{2,1,0:T(8,128)S(1)} all-to-all(f32[8,8,128]{2,1,0:T(8,128)S(1)} %bitcast.38), channel_id=1, replica_groups=mesh['win'=8,'obs'=32] {'win'}, dimensions={0} | all-to-all | bytes 65536 | tf_op jit(solution)/shard_map/all_to_all | solution.py:264
  143.5 0.4 solve.5
  143.9 11.6 %all_to_all.107 = f32[32,1,128]{2,1,0:T(1,128)S(1)} all-to-all(f32[32,1,128]{2,1,0:T(1,128)S(1)} %bitcast.46), channel_id=1, replica_groups=mesh['win'=8,'obs'=32] {'obs'}, dimensions={0} | all-to-all | bytes 32768 | tf_op jit(solution)/shard_map/all_to_all | solution.py:266
  155.5 5.3 %correct.1 = (f32[8,300]{1,0:T(8,128)}, f32[1,32768]{1,0:T(1,128)}) custom-call(f32[8,32768]{1,0:T(8,128)S(1)} %bitcast.29, f32[1,32768]{1,0:T(1,128)S(1)} %copy-done.2, s32[1,32768]{1,0:T(1,128)S(1)} %copy-done.3, f32[32,128]{1,0:T(8,128)S(1)} %bitcast.47), custom_call_target="tpu_custom_call" | custom-call | tf_op jit(solution)/shard_map/correct/pallas_call | solution.py:232
Async XLA Ops:
  0.6 1.2 copy-start
  1.9 0.9 copy-start.2
  2.8 0.9 copy-start.3
  3.7 54.8 %copy-start.1 = (f32[1,8,32768]{2,1,0:T(8,128)S(1)}, f32[1,8,32768]{2,1,0:T(8,128)}, u32[]{:S(2)}) copy-start(f32[1,8,32768]{2,1,0:T(8,128)} %param.5) | copy-start | bytes 3145732
  34.1 0.7 copy-start.5
  45.7 0.7 copy-start.4
where the time goes:
time: 161 us
  blocking collectives  111 us (69%)
  Pallas kernels  45.1 us (28%)
  local copies, waits for them, and re-layouts  4.39 us (3%)
    pallas_call x10, Pallas kernels, call(): pl.pallas_call(kernel, name=name, out_shape=out_shape, in_specs=[vmem] *...  45.1 us
    all_to_all x3, blocking collectives, body(): parts = lax.all_to_all(parts, 'obs', 0, 0, tiled=True)  44.3 us
    all_to_all x3, blocking collectives, body(): got = lax.all_to_all(flat, 'obs', 0, 0, tiled=True)  34.8 us
    all_to_all x3, blocking collectives, body(): tiles = lax.all_to_all(tile, 'win', 0, 0, tiled=True)  31.5 us
    unnamed x12, local copies, waits for them, and re-layouts  4.39 us

commit v1 on v0

--- a/solution.py
+++ b/solution.py
@@ -17,7 +17,7 @@
 HALF = 5
 SPLIT = HALF * OWNERS
 FEATS = 48
-CHUNK = 1024
+CHUNK = 16384
 
 
 def channel_row(ref):
@@ -69,18 +69,35 @@
     return jnp.sum(jnp.concatenate(parts, axis=1), axis=0, keepdims=True)
 
 
+def fetch(sources, targets, sems):
+    copies = []
+    for t in range(targets[0].shape[1] // CHUNK):
+        at = pl.ds(t * CHUNK, CHUNK)
+        chunk = [
+            pltpu.make_async_copy(source.at[:, at], target.at[:, at], sems.at[t, n])
+            for n, (source, target) in enumerate(zip(sources, targets))
+        ]
+        for copy in chunk:
+            copy.start()
+        copies.append(chunk)
+    return copies
+
+
 def statistics_kernel(first, *refs):
     if first:
-        pred_ref, dep_ref, chan_ref, out_ref, acc_ref = refs
+        *sources, out_ref, pred_ref, dep_ref, chan_ref, sems = refs
+        copies = fetch(sources, (pred_ref, dep_ref, chan_ref), sems)
     else:
-        pred_ref, dep_ref, chan_ref, got_ref, out_ref, acc_ref = refs
+        pred_ref, dep_ref, chan_ref, got_ref, out_ref = refs
         tables = build_tables(got_ref)
-    total = pred_ref.shape[1]
-    acc_ref[...] = jnp.zeros_like(acc_ref)
     row_id = lax.broadcasted_iota(jnp.int32, (SPLIT, CHUNK), 0)
 
-    def step(i, carry):
-        at = pl.ds(pl.multiple_of(i * CHUNK, CHUNK), CHUNK)
+    sums = jnp.zeros((4 * FEATS, SPLIT), jnp.float32)
+    for start in range(0, pred_ref.shape[1], CHUNK):
+        at = slice(start, start + CHUNK)
+        if first:
+            for copy in copies[start // CHUNK]:
+                copy.wait()
         p = pred_ref[:, at]
         d = dep_ref[:, at]
         c = chan_ref[:, at]
@@ -102,16 +119,20 @@
         )
         local = jnp.where(upper, c - SPLIT, c)
         hot = (row_id == local).astype(jnp.float32).astype(jnp.bfloat16)
-        acc_ref[...] += lax.dot_general(
-            hot, columns, (((1,), (1,)), ((), ())), preferred_element_type=jnp.float32
+        sums = sums + lax.dot_general(
+            columns, hot, (((1,), (1,)), ((), ())), preferred_element_type=jnp.float32
         )
-        return carry
-
-    lax.fori_loop(0, total // CHUNK, step, 0)
+
     wide = 2 * FEATS
-    sums = acc_ref[:, :wide] + acc_ref[:, wide:]
-    sums = jnp.concatenate([sums, jnp.zeros((SPLIT, LANES - wide), jnp.float32)], axis=1)
-    last = sums[4 * OWNERS :, :]
+    sums = sums[:wide, :] + sums[wide:, :]
+    sums = jnp.concatenate(
+        [
+            jnp.concatenate([sums, jnp.zeros((wide, 2 * LANES - SPLIT), jnp.float32)], axis=1),
+            jnp.zeros((LANES - wide, 2 * LANES), jnp.float32),
+        ],
+        axis=0,
+    ).T
+    last = sums[4 * OWNERS : 5 * OWNERS, :]
     lane = lax.broadcasted_iota(jnp.int32, (OWNERS, LANES), 1)
     for j in range(4):
         rows = sums[j * OWNERS : (j + 1) * OWNERS, :]
@@ -218,25 +239,22 @@
         stop = min((t + 1) * LANES, count)
         coef_ref[:, t * LANES : stop] = tables[t][:, : stop - t * LANES]
 
-    def step(i, carry):
-        at = pl.ds(pl.multiple_of(i * CHUNK, CHUNK), CHUNK)
+    for start in range(0, pred_ref.shape[1], CHUNK):
+        at = slice(start, start + CHUNK)
         out_ref[:, at] = dep_ref[:, at] - fit(pred_ref[:, at], chan_ref[:, at], tables)
-        return carry
-
-    lax.fori_loop(0, pred_ref.shape[1] // CHUNK, step, 0)
-
-
-def call(kernel, name, out_shape, operands, scratch=()):
+
+
+def call(kernel, name, out_shape, operands, scratch=(), space=pltpu.VMEM, limit=32):
     vmem = pl.BlockSpec(memory_space=pltpu.VMEM)
     several = isinstance(out_shape, list)
     return pl.pallas_call(
         kernel,
         name=name,
         out_shape=out_shape,
-        in_specs=[vmem] * len(operands),
+        in_specs=[pl.BlockSpec(memory_space=space)] * len(operands),
         out_specs=[vmem] * len(out_shape) if several else vmem,
         scratch_shapes=list(scratch),
-        compiler_params=pltpu.CompilerParams(vmem_limit_bytes=32 << 20),
+        compiler_params=pltpu.CompilerParams(vmem_limit_bytes=limit << 20),
     )(*operands)
 
 
@@ -251,14 +269,16 @@
     windows = lax.axis_size("win")
     got = None
     for _ in range(ROUNDS):
-        operands = [rows_here, departures, channel] + ([] if got is None else [got])
-        parts = call(
-            functools.partial(statistics_kernel, got is None),
-            "statistics",
-            shape(4 * OWNERS, LANES),
-            operands,
-            [pltpu.VMEM((SPLIT, 4 * FEATS), jnp.float32)],
-        )
+        operands = [rows_here, departures, channel]
+        out = shape(4 * OWNERS, LANES)
+        if got is None:
+            scratch = [pltpu.VMEM(x.shape, x.dtype) for x in operands]
+            scratch.append(pltpu.SemaphoreType.DMA((total // CHUNK, len(operands))))
+            kernel = functools.partial(statistics_kernel, True)
+            parts = call(kernel, "statistics", out, operands, scratch, pl.ANY, 62)
+        else:
+            kernel = functools.partial(statistics_kernel, False)
+            parts = call(kernel, "statistics", out, [*operands, got])
         parts = lax.all_to_all(parts, "obs", 0, 0, tiled=True)
         tile = call(reduce_kernel, "reduce", shape(windows * SUB, LANES), [parts, decay_rate])
         tiles = lax.all_to_all(tile, "win", 0, 0, tiled=True)

time: 161 us -> 134 us (0.83)
  Pallas kernels: 45.1 us -> 20.6 us
  local copies, waits for them, and re-layouts: 4.39 us -> 0.7 us
    pallas_call x10, Pallas kernels: 45.1 us -> 20.6 us  [call(): pl.pallas_call(kernel, name=name, out_shape=out_shape, in_specs=[pl.Block...]
    unnamed x12 -> x10, local copies, waits for them, and re-layouts: 4.39 us -> 0.7 us
where the time goes in v1:
time: 134 us; the launch traced here: 133 us
  blocking collectives  111 us (83%)
  Pallas kernels  20.6 us (15%)
    all_to_all x3, blocking collectives, body(): parts = lax.all_to_all(parts, 'obs', 0, 0, tiled=True)  44.7 us
    all_to_all x3, blocking collectives, body(): got = lax.all_to_all(flat, 'obs', 0, 0, tiled=True)  35 us
    all_to_all x3, blocking collectives, body(): tiles = lax.all_to_all(tile, 'win', 0, 0, tiled=True)  31.5 us
    pallas_call x10, Pallas kernels, call(): pl.pallas_call(kernel, name=name, out_shape=out_shape, in_specs=[pl.Block...  20.6 us

profile of v1, /device:TPU:1, one launch (start us, length us, event | category | flops | bytes accessed | tf_op | source)
XLA Modules:
  0.0 133.1 jit_solution(4003020013771186338)
XLA Ops:
  0.6 0.0 copy-start
  0.6 7.8 %statistics.3 = f32[128,128]{1,0:T(8,128)} custom-call(f32[8,32768]{1,0:T(8,128)} %bitcast.26, f32[1,32768]{1,0:T(1,128)} %dep_ref.1, s32[1,32768]{1,0:T(1,128)} %chan_ref.1), custom_call_target="tpu_custom_call" | custom-call | tf_op jit(solution)/shard_map/statistics/pallas_call | solution.py:250
  8.5 0.0 copy-start.4
  8.5 0.0 copy-start.2
  8.5 21.0 %all_to_all.99 = f32[32,4,128]{2,1,0:T(4,128)S(1)} all-to-all(f32[32,4,128]{2,1,0:T(4,128)} %bitcast.47), channel_id=1, replica_groups=mesh['win'=8,'obs'=32] {'obs'}, dimensions={0} | all-to-all | bytes 131072 | tf_op jit(solution)/shard_map/all_to_all | solution.py:282
  29.5 0.0 copy-start.1
  29.5 0.0 copy-done.4
  29.5 0.1 reduce.3
  29.6 10.9 %all_to_all.100 = f32[8,8,128]{2,1,0:T(8,128)S(1)} all-to-all(f32[8,8,128]{2,1,0:T(8,128)S(1)} %bitcast.35), channel_id=1, replica_groups=mesh['win'=8,'obs'=32] {'win'}, dimensions={0} | all-to-all | bytes 65536 | tf_op jit(solution)/shard_map/all_to_all | solution.py:284
  40.5 0.0 copy-start.3
  40.5 0.7 copy-done.3
  41.2 0.4 solve.3
  41.6 11.6 %all_to_all.101 = f32[32,1,128]{2,1,0:T(1,128)S(1)} all-to-all(f32[32,1,128]{2,1,0:T(1,128)S(1)} %bitcast.43), channel_id=1, replica_groups=mesh['win'=8,'obs'=32] {'obs'}, dimensions={0} | all-to-all | bytes 32768 | tf_op jit(solution)/shard_map/all_to_all | solution.py:286
  53.2 0.0 copy-done
  53.2 0.0 copy-done.2
  53.2 0.0 copy-done.1
  53.2 4.3 %statistics.4 = f32[128,128]{1,0:T(8,128)S(1)} custom-call(f32[8,32768]{1,0:T(8,128)S(1)} %bitcast.27, f32[1,32768]{1,0:T(1,128)S(1)} %copy-done.1, s32[1,32768]{1,0:T(1,128)S(1)} %copy-done.2, f32[32,128]{1,0:T(8,128)S(1)} %bitcast.41), custom_call_target="tpu_custom_call" | custom-call | tf_op jit(solution)/shard_map/statistics/pallas_call | solution.py:250
  57.6 11.8 %all_to_all.102 = f32[32,4,128]{2,1,0:T(4,128)S(1)} all-to-all(f32[32,4,128]{2,1,0:T(4,128)S(1)} %bitcast.30), channel_id=1, replica_groups=mesh['win'=8,'obs'=32] {'obs'}, dimensions={0} | all-to-all | bytes 131072 | tf_op jit(solution)/shard_map/all_to_all | solution.py:282
  69.4 0.1 reduce.4
  69.5 10.3 %all_to_all.103 = f32[8,8,128]{2,1,0:T(8,128)S(1)} all-to-all(f32[8,8,128]{2,1,0:T(8,128)S(1)} %bitcast.36), channel_id=1, replica_groups=mesh['win'=8,'obs'=32] {'win'}, dimensions={0} | all-to-all | bytes 65536 | tf_op jit(solution)/shard_map/all_to_all | solution.py:284
  79.8 0.4 solve.4
  80.2 11.8 %all_to_all.104 = f32[32,1,128]{2,1,0:T(1,128)S(1)} all-to-all(f32[32,1,128]{2,1,0:T(1,128)S(1)} %bitcast.44), channel_id=1, replica_groups=mesh['win'=8,'obs'=32] {'obs'}, dimensions={0} | all-to-all | bytes 32768 | tf_op jit(solution)/shard_map/all_to_all | solution.py:286
  92.0 4.3 %statistics.5 = f32[128,128]{1,0:T(8,128)S(1)} custom-call(f32[8,32768]{1,0:T(8,128)S(1)} %bitcast.28, f32[1,32768]{1,0:T(1,128)S(1)} %copy-done.1, s32[1,32768]{1,0:T(1,128)S(1)} %copy-done.2, f32[32,128]{1,0:T(8,128)S(1)} %bitcast.42), custom_call_target="tpu_custom_call" | custom-call | tf_op jit(solution)/shard_map/statistics/pallas_call | solution.py:250
  96.3 11.8 %all_to_all.105 = f32[32,4,128]{2,1,0:T(4,128)S(1)} all-to-all(f32[32,4,128]{2,1,0:T(4,128)S(1)} %bitcast.31), channel_id=1, replica_groups=mesh['win'=8,'obs'=32] {'obs'}, dimensions={0} | all-to-all | bytes 131072 | tf_op jit(solution)/shard_map/all_to_all | solution.py:282
  108.1 0.1 reduce.5
  108.2 10.3 %all_to_all.106 = f32[8,8,128]{2,1,0:T(8,128)S(1)} all-to-all(f32[8,8,128]{2,1,0:T(8,128)S(1)} %bitcast.37), channel_id=1, replica_groups=mesh['win'=8,'obs'=32] {'win'}, dimensions={0} | all-to-all | bytes 65536 | tf_op jit(solution)/shard_map/all_to_all | solution.py:284
  118.5 0.4 solve.5
  118.9 11.6 %all_to_all.107 = f32[32,1,128]{2,1,0:T(1,128)S(1)} all-to-all(f32[32,1,128]{2,1,0:T(1,128)S(1)} %bitcast.45), channel_id=1, replica_groups=mesh['win'=8,'obs'=32] {'obs'}, dimensions={0} | all-to-all | bytes 32768 | tf_op jit(solution)/shard_map/all_to_all | solution.py:286
  130.5 2.6 %correct.1 = (f32[8,300]{1,0:T(8,128)}, f32[1,32768]{1,0:T(1,128)}) custom-call(f32[8,32768]{1,0:T(8,128)S(1)} %bitcast.29, f32[1,32768]{1,0:T(1,128)S(1)} %copy-done.1, s32[1,32768]{1,0:T(1,128)S(1)} %copy-done.2, f32[32,128]{1,0:T(8,128)S(1)} %bitcast.46), custom_call_target="tpu_custom_call" | custom-call | tf_op jit(solution)/shard_map/correct/pallas_call | solution.py:250
Async XLA Ops:
  0.6 52.6 %copy-start = (f32[1,8,32768]{2,1,0:T(8,128)S(1)}, f32[1,8,32768]{2,1,0:T(8,128)}, u32[]{:S(2)}) copy-start(f32[1,8,32768]{2,1,0:T(8,128)} %param.5) | copy-start | bytes 3145732
  8.5 21.1 %copy-start.4 = (f32[1,300]{1,0:T(1,128)S(1)}, f32[1,300]{1,0:T(1,128)}, u32[]{:S(2)}) copy-start(f32[1,300]{1,0:T(1,128)} %decay_ref.5) | copy-start | bytes 3604
  8.5 44.8 %copy-start.2 = (s32[1,32768]{1,0:T(1,128)S(1)}, s32[1,32768]{1,0:T(1,128)}, u32[]{:S(2)}) copy-start(s32[1,32768]{1,0:T(1,128)} %chan_ref.1) | copy-start | bytes 393220
  29.5 23.7 %copy-start.1 = (f32[1,32768]{1,0:T(1,128)S(1)}, f32[1,32768]{1,0:T(1,128)}, u32[]{:S(2)}) copy-start(f32[1,32768]{1,0:T(1,128)} %dep_ref.1) | copy-start | bytes 393220
  40.5 0.7 copy-start.3

commit v2 on v1

v2 whole, which is shorter than its diff:
```python
import functools

import jax
import jax.numpy as jnp
from jax import lax
from jax.experimental import pallas as pl
from jax.experimental.pallas import tpu as pltpu
from jax.sharding import PartitionSpec as P

ROUNDS = 3
EDGE = 1.5

LANES = 128
SUB = 8
XS, CORES, YS, ZS = 4, 2, 4, 8
BLOCKS = CORES * ZS
SLOTS = 20
HALF = 10
SPLIT = HALF * BLOCKS
FEATS = 48
WIDE = 2 * FEATS
CHUNK = 16384

NEAR = [
    [(CORES * x + c) * YS * ZS + ZS * y + z for c in range(CORES) for z in range(ZS)]
    for x in range(XS)
    for y in range(YS)
]
ACROSS = [
    [(CORES * x + c) * YS * ZS + ZS * y + z for x in range(XS) for y in range(YS)]
    for c in range(CORES)
    for z in range(ZS)
]


def iotas(rows=SUB):
    row = lax.broadcasted_iota(jnp.int32, (rows, LANES), 0)
    lane = lax.broadcasted_iota(jnp.int32, (rows, LANES), 1)
    return row, lane


def take(table, index):
    return jnp.take_along_axis(table, index, axis=1, mode="promise_in_bounds")


def spread(x, i):
    return jnp.broadcast_to(x[i : i + 1, :], (SUB, LANES))


def channel_tables(ref):
    count = ref.shape[1]
    tables = []
    for start in range(0, 3 * LANES, LANES):
        stop = min(start + LANES, count)
        row = ref[:, start:stop].astype(jnp.float32)
        if stop - start < LANES:
            fill = jnp.ones((1, LANES - (stop - start)), jnp.float32)
            row = jnp.concatenate([row, fill], axis=1)
        tables.append(jnp.broadcast_to(row, (SUB, LANES)))
    return tables


def pick(tables, index):
    low = index & (LANES - 1)
    first, second, third = [take(t, low) for t in tables]
    return jnp.where(index < LANES, first, jnp.where(index < 2 * LANES, second, third))


def build_tables(got_ref):
    square = jnp.concatenate(
        [got_ref[pl.ds(r, BLOCKS, stride=2), :] for r in range(2)]
        + [jnp.zeros((LANES - 2 * BLOCKS, LANES), jnp.float32)],
        axis=0,
    ).T
    _, lane = iotas()
    tables = []
    for t in range(3):
        table = jnp.zeros((SUB, LANES), jnp.float32)
        for q in range(SUB):
            slot = SUB * t + q
            if slot >= SLOTS:
                continue
            r, s = divmod(slot, BLOCKS)
            tile = square[s * SUB : (s + 1) * SUB, :]
            shift = (q - r) * BLOCKS % LANES
            if shift:
                tile = pltpu.roll(tile, shift, 1)
            table = jnp.where((lane >> 4) == q, tile, table)
        tables.append(table)
    return tables


def fit(predictors, channels, tables):
    parts = []
    for g in range(predictors.shape[1] // LANES):
        at = slice(g * LANES, (g + 1) * LANES)
        index = jnp.broadcast_to(channels[:, at], (SUB, LANES))
        parts.append(predictors[:, at] * pick(tables, index))
    return jnp.sum(jnp.concatenate(parts, axis=1), axis=0, keepdims=True)


def block_rows(ref):
    tables = channel_tables(ref)
    row, lane = iotas()
    slot = jnp.clip(lane - WIDE, 0, SLOTS - 1)
    return jnp.concatenate(
        [pick(tables, slot * BLOCKS + row + half) for half in range(0, BLOCKS, SUB)], axis=0
    )


def statistics_kernel(first, *refs):
    if first:
        *sources, out_ref, pred_ref, dep_ref, chan_ref, decay_ref, ridge_ref, sems = refs
        targets = (pred_ref, dep_ref, chan_ref, decay_ref, ridge_ref)
        copies = [
            pltpu.make_async_copy(source, target, sems.at[n])
            for n, (source, target) in enumerate(zip(sources, targets))
        ]
        for copy in copies:
            copy.start()
        for copy in copies:
            copy.wait()
    else:
        pred_ref, dep_ref, chan_ref, decay_ref, ridge_ref, got_ref, out_ref = refs
        tables = build_tables(got_ref)
    row_id = lax.broadcasted_iota(jnp.int32, (SPLIT, CHUNK), 0)

    sums = jnp.zeros((2 * WIDE, SPLIT), jnp.float32)
    for start in range(0, pred_ref.shape[1], CHUNK):
        at = slice(start, start + CHUNK)
        p = pred_ref[:, at]
        d = dep_ref[:, at]
        c = chan_ref[:, at]
        residual = d if first else d - fit(p, c, tables)
        weight = EDGE / jnp.maximum(jnp.abs(residual), EDGE)
        wp = p * weight
        rows = [wp * p]
        for offset in range(1, 5):
            rows.append(wp * pltpu.roll(p, SUB - offset, 0))
        rows.append(wp * d)
        feats = jnp.concatenate(rows, axis=0)
        head = feats.astype(jnp.bfloat16)
        tail = (feats - head.astype(jnp.float32)).astype(jnp.bfloat16)
        upper = c >= SPLIT
        in_upper = upper.astype(jnp.float32).astype(jnp.bfloat16)
        in_lower = 1.0 - in_upper
        columns = jnp.concatenate(
            [head * in_lower, head * in_upper, tail * in_lower, tail * in_upper], axis=0
        )
        local = jnp.where(upper, c - SPLIT, c)
        hot = (row_id == local).astype(jnp.float32).astype(jnp.bfloat16)
        sums = sums + lax.dot_general(
            columns, hot, (((1,), (1,)), ((), ())), preferred_element_type=jnp.float32
        )

    sums = sums[:WIDE, :] + sums[WIDE:, :]
    sums = jnp.concatenate(
        [
            jnp.concatenate([sums, jnp.zeros((WIDE, 2 * LANES - SPLIT), jnp.float32)], axis=1),
            jnp.zeros((LANES - WIDE, 2 * LANES), jnp.float32),
        ],
        axis=0,
    ).T
    _, lane = iotas(BLOCKS)
    for j in range(SUB):
        if j < 6:
            q, third = divmod(j, 3)
            spill = sums[(SUB + q) * BLOCKS : (SUB + q + 1) * BLOCKS, :]
            spill = pltpu.roll(spill, WIDE - 32 * third, 1)
        else:
            spill = block_rows(decay_ref if j == 6 else ridge_ref)
        rows = jnp.where(lane < WIDE, sums[j * BLOCKS : (j + 1) * BLOCKS, :], spill)
        out_ref[pl.ds(j, BLOCKS, stride=SUB), :] = rows


def is_side():
    row, lane = iotas()
    return (row >= 6) & (lane >= WIDE)


def add_tiles(ref, starts):
    tiles = [ref[s : s + SUB, :] for s in starts]
    total = tiles[0]
    for tile in tiles[1:]:
        total = total + tile
    return jnp.where(is_side(), tiles[0], total)


def reduce_kernel(parts_ref, out_ref):
    for i in range(CORES):
        tile = add_tiles(parts_ref, [(i * ZS + z) * SUB for z in range(ZS)])
        for p in range(XS * YS):
            at = (p * CORES + i) * SUB
            out_ref[at : at + SUB, :] = tile


def solve_kernel(all_ref, out_ref):
    here = lax.axis_index("win") // CORES
    row, lane = iotas()

    spilled = lane >= WIDE
    third = jnp.where(row < 3, row, row - 3)
    column = jnp.where(spilled, 32 * third + lane - WIDE, lane)
    j = jnp.where(spilled, jnp.where(row < 3, SUB, SUB + 1), row)
    slot = jnp.where(column >= FEATS, HALF, 0) + j

    carried = jnp.zeros((SUB, LANES), jnp.float32)
    kept = [carried, carried]
    side = [carried, carried]
    for x in range(XS):
        for i in range(CORES):
            tile = add_tiles(all_ref, [((x * YS + y) * CORES + i) * SUB for y in range(YS)])
            carried = take(spread(tile, 6), WIDE + slot) * carried + tile
            kept[i] = jnp.where(here == x, carried, kept[i])
            side[i] = jnp.where(here == x, tile, side[i])

    tiles = []
    for i in range(CORES):
        turned = [pltpu.roll(kept[i], (32 * t + LANES - WIDE) % LANES, 1) for t in range(3)]
        extra = []
        for q in range(2):
            a, b, c = [pltpu.roll(turned[t], (q - 3 * q - t) % SUB, 0) for t in range(3)]
            extra.append(jnp.where(lane < 32, a, jnp.where(lane < 64, b, c)))
        tiles.append(kept[i])
        tiles.append(jnp.where(row == 0, extra[0], jnp.where(row == 1, extra[1], 0.0)))
    square = jnp.concatenate(
        tiles + [jnp.zeros((LANES - 2 * CORES * SUB, LANES), jnp.float32)], axis=0
    ).T
    blocks = []
    for b in range(6):
        low = square[b * SUB : (b + 1) * SUB, :]
        high = square[FEATS + b * SUB : FEATS + (b + 1) * SUB, :]
        blocks.append(jnp.where(lane < 32, low, pltpu.roll(high, 32, 1)))

    slot = jnp.where((lane & 32) == 0, 0, HALF) + jnp.minimum(lane & 15, HALF - 1)
    ridges = [take(spread(s, 7), WIDE + slot) for s in side]
    ridge = jnp.where((lane & 16) == 0, ridges[0], ridges[1])

    offsets = blocks[:5]
    for d in range(5, SUB):
        offsets.append(pltpu.roll(blocks[SUB - d], SUB - d, 0))
    offsets[0] = offsets[0] + ridge
    columns = []
    for j in range(SUB):
        column = offsets[0]
        for d in range(1, SUB):
            column = jnp.where(row == (j - d) % SUB, offsets[d], column)
        columns.append(column)

    right = blocks[5]
    inverse = jnp.ones((SUB, LANES), jnp.float32)
    for j in range(SUB):
        inv = 1.0 / spread(columns[j], j)
        inverse = jnp.where(row == j, inv, inverse)
        factor = jnp.where(row > j, columns[j] * inv, 0.0)
        for k in range(j + 1, SUB):
            columns[k] = columns[k] - factor * spread(columns[k], j)
        right = right - factor * spread(right, j)
    answer = right * inverse
    for j in range(SUB - 1, 0, -1):
        factor = jnp.where(row < j, columns[j] * inverse, 0.0)
        answer = answer - factor * spread(answer, j)

    for i in range(CORES):
        flats = []
        for r in range(2):
            slot = jnp.minimum(BLOCKS * r + (lane >> 3), SLOTS - 1)
            source = jnp.where(slot >= HALF, slot - HALF + 32, slot) + 16 * i
            flat = jnp.where(row == (lane & 7), take(answer, source), 0.0)
            flats.append(jnp.sum(flat, axis=0, keepdims=True))
        tile = jnp.where((row & 1) == 0, flats[0], flats[1])
        for half in range(2):
            at = (2 * i + half) * SUB
            out_ref[at : at + SUB, :] = tile


def correct_kernel(pred_ref, dep_ref, chan_ref, got_ref, coef_ref, out_ref):
    tables = build_tables(got_ref)
    count = coef_ref.shape[1]
    for t in range(3):
        stop = min((t + 1) * LANES, count)
        coef_ref[:, t * LANES : stop] = tables[t][:, : stop - t * LANES]

    for start in range(0, pred_ref.shape[1], CHUNK):
        at = slice(start, start + CHUNK)
        out_ref[:, at] = dep_ref[:, at] - fit(pred_ref[:, at], chan_ref[:, at], tables)


def call(kernel, name, out_shape, operands, scratch=(), space=pltpu.VMEM, limit=32):
    vmem = pl.BlockSpec(memory_space=pltpu.VMEM)
    several = isinstance(out_shape, list)
    return pl.pallas_call(
        kernel,
        name=name,
        out_shape=out_shape,
        in_specs=[pl.BlockSpec(memory_space=space)] * len(operands),
        out_specs=[vmem] * len(out_shape) if several else vmem,
        scratch_shapes=list(scratch),
        compiler_params=pltpu.CompilerParams(vmem_limit_bytes=limit << 20),
    )(*operands)


def shape(*dims):
    return jax.ShapeDtypeStruct(dims, jnp.float32)


def exchange(x, groups):
    return lax.all_to_all(
        x, ("win", "obs"), 0, 0, tiled=True, axis_index_groups=groups
    )


def body(predictors, departures, channel, decay_rate, ridge_counts):
    observed = [predictors[0], departures, channel]
    operands = [*observed, decay_rate, ridge_counts]
    total = departures.shape[1]
    out = shape(BLOCKS * SUB, LANES)
    got = None
    for _ in range(ROUNDS):
        if got is None:
            scratch = [pltpu.VMEM(x.shape, x.dtype) for x in operands]
            scratch.append(pltpu.SemaphoreType.DMA((len(operands),)))
            kernel = functools.partial(statistics_kernel, True)
            parts = call(kernel, "statistics", out, operands, scratch, pl.ANY, 62)
        else:
            kernel = functools.partial(statistics_kernel, False)
            parts = call(kernel, "statistics", out, [*operands, got])
        parts = exchange(parts, NEAR)
        pair = call(reduce_kernel, "reduce", shape(XS * YS * CORES * SUB, LANES), [parts])
        tiles = exchange(pair, ACROSS)
        flat = call(solve_kernel, "solve", shape(2 * BLOCKS, LANES), [tiles])
        got = exchange(flat, NEAR)
    coeffs, corrected = call(
        correct_kernel,
        "correct",
        [shape(SUB, decay_rate.shape[1]), shape(1, total)],
        [*observed, got],
    )
    return (coeffs[None], corrected)


def solution(mesh):
    placed = (
        P("win", None, "obs"),
        P("win", "obs"),
        P("win", "obs"),
        P("win", None),
        P("win", None),
    )
    return jax.shard_map(
        body,
        mesh=mesh,
        in_specs=placed,
        out_specs=(P("win", None, None), P("win", "obs")),
        check_vma=False,
    )
```

time: 134 us -> 126 us (0.940)
  blocking collectives: 111 us -> 106 us
  Pallas kernels: 20.6 us -> 18.2 us
    all_to_all x9, blocking collectives: 111 us -> 106 us  [exchange(): lax.all_to_all(x, ('win', 'obs'), 0, 0, tiled=True, axis_index_groups=gro...]
    pallas_call x10, Pallas kernels: 20.6 us -> 18.2 us  [call(): pl.pallas_call(kernel, name=name, out_shape=out_shape, in_specs=[pl.Block...]
where the time goes in v2:
time: 126 us
  blocking collectives  106 us (84%)
  Pallas kernels  18.2 us (14%)
    all_to_all x9, blocking collectives, exchange(): lax.all_to_all(x, ('win', 'obs'), 0, 0, tiled=True, axis_index_groups=gro...  106 us
    pallas_call x10, Pallas kernels, call(): pl.pallas_call(kernel, name=name, out_shape=out_shape, in_specs=[pl.Block...  18.2 us

profile of v2, /device:TPU:1, one launch (start us, length us, event | category | flops | bytes accessed | tf_op | source)
XLA Modules:
  0.0 125.6 jit_solution(9342776507060027348)
XLA Ops:
  0.6 0.0 copy-start
  0.6 5.6 %statistics.3 = f32[128,128]{1,0:T(8,128)} custom-call(f32[8,32768]{1,0:T(8,128)} %bitcast.20, f32[1,32768]{1,0:T(1,128)} %dep_ref.1, s32[1,32768]{1,0:T(1,128)} %chan_ref.1, f32[1,300]{1,0:T(1,128)} %refs_3_.5, s32[1,300]{1,0:T(1,128)} %refs_4_.5), custom_call_target="tpu_custom_call" | custom-call | tf_op jit(solution)/shard_map/statistics/pallas_call | solution.py:292
  6.2 17.2 %all_to_all.99 = f32[16,8,128]{2,1,0:T(8,128)S(1)} all-to-all(f32[16,8,128]{2,1,0:T(8,128)} %bitcast.41), channel_id=1, replica_groups={{0,1,2,3,4,5,6,7,32,33,34,35,36,37,38,39},{8,9,10,11,12,13,14,15,40,41,..., dimensions={0} | all-to-all | bytes 131072 | tf_op jit(solution)/shard_map/all_to_all | solution.py:308
  23.4 0.0 copy-start.2
  23.4 13.4 %all_to_all.100 = f32[16,16,128]{2,1,0:T(8,128)S(1)} all-to-all(f32[16,16,128]{2,1,0:T(8,128)S(1)} %bitcast.24), channel_id=1, replica_groups={{0,8,16,24,64,72,80,88,128,136,144,152,192,200,208,216},{1,9,17,25,65,7..., dimensions={0} | all-to-all | bytes 262144 | tf_op jit(solution)/shard_map/all_to_all | solution.py:308
  36.8 0.0 copy-start.1
  36.8 0.5 solve.3
  37.3 0.0 copy-start.4
  37.3 11.7 %all_to_all.101 = f32[16,2,128]{2,1,0:T(2,128)S(1)} all-to-all(f32[16,2,128]{2,1,0:T(2,128)S(1)} %bitcast.37), channel_id=1, replica_groups={{0,1,2,3,4,5,6,7,32,33,34,35,36,37,38,39},{8,9,10,11,12,13,14,15,40,41,..., dimensions={0} | all-to-all | bytes 32768 | tf_op jit(solution)/shard_map/all_to_all | solution.py:308
  49.0 0.0 copy-start.3
  49.0 0.0 copy-done
  49.0 0.0 copy-done.2
  49.0 0.0 copy-done.1
  49.1 0.0 copy-done.4
  49.1 0.7 copy-done.3
  49.7 4.2 %statistics.4 = f32[128,128]{1,0:T(8,128)S(1)} custom-call(f32[8,32768]{1,0:T(8,128)S(1)} %bitcast.21, f32[1,32768]{1,0:T(1,128)S(1)} %copy-done.1, s32[1,32768]{1,0:T(1,128)S(1)} %copy-done.2, f32[1,300]{1,0:T(1,128)S(1)} %copy-done.3, s32[1,300]{1,0:T(1,128)S(1)} %copy-done.4, f32[32,128]{1,0:T(8,128)S(1)} %bitcast.35), custom_call_target="tpu_custom_call" | custom-call | tf_op jit(solution)/shard_map/statistics/pallas_call | solution.py:292
  54.0 10.3 %all_to_all.102 = f32[16,8,128]{2,1,0:T(8,128)S(1)} all-to-all(f32[16,8,128]{2,1,0:T(8,128)S(1)} %bitcast.31), channel_id=1, replica_groups={{0,1,2,3,4,5,6,7,32,33,34,35,36,37,38,39},{8,9,10,11,12,13,14,15,40,41,..., dimensions={0} | all-to-all | bytes 131072 | tf_op jit(solution)/shard_map/all_to_all | solution.py:308
  64.3 9.8 %all_to_all.103 = f32[16,16,128]{2,1,0:T(8,128)S(1)} all-to-all(f32[16,16,128]{2,1,0:T(8,128)S(1)} %bitcast.26), channel_id=1, replica_groups={{0,8,16,24,64,72,80,88,128,136,144,152,192,200,208,216},{1,9,17,25,65,7..., dimensions={0} | all-to-all | bytes 262144 | tf_op jit(solution)/shard_map/all_to_all | solution.py:308
  74.1 0.5 solve.4
  74.7 11.7 %all_to_all.104 = f32[16,2,128]{2,1,0:T(2,128)S(1)} all-to-all(f32[16,2,128]{2,1,0:T(2,128)S(1)} %bitcast.38), channel_id=1, replica_groups={{0,1,2,3,4,5,6,7,32,33,34,35,36,37,38,39},{8,9,10,11,12,13,14,15,40,41,..., dimensions={0} | all-to-all | bytes 32768 | tf_op jit(solution)/shard_map/all_to_all | solution.py:308
  86.4 4.2 %statistics.5 = f32[128,128]{1,0:T(8,128)S(1)} custom-call(f32[8,32768]{1,0:T(8,128)S(1)} %bitcast.22, f32[1,32768]{1,0:T(1,128)S(1)} %copy-done.1, s32[1,32768]{1,0:T(1,128)S(1)} %copy-done.2, f32[1,300]{1,0:T(1,128)S(1)} %copy-done.3, s32[1,300]{1,0:T(1,128)S(1)} %copy-done.4, f32[32,128]{1,0:T(8,128)S(1)} %bitcast.36), custom_call_target="tpu_custom_call" | custom-call | tf_op jit(solution)/shard_map/statistics/pallas_call | solution.py:292
  90.6 10.3 %all_to_all.105 = f32[16,8,128]{2,1,0:T(8,128)S(1)} all-to-all(f32[16,8,128]{2,1,0:T(8,128)S(1)} %bitcast.33), channel_id=1, replica_groups={{0,1,2,3,4,5,6,7,32,33,34,35,36,37,38,39},{8,9,10,11,12,13,14,15,40,41,..., dimensions={0} | all-to-all | bytes 131072 | tf_op jit(solution)/shard_map/all_to_all | solution.py:308
  101.0 9.8 %all_to_all.106 = f32[16,16,128]{2,1,0:T(8,128)S(1)} all-to-all(f32[16,16,128]{2,1,0:T(8,128)S(1)} %bitcast.28), channel_id=1, replica_groups={{0,8,16,24,64,72,80,88,128,136,144,152,192,200,208,216},{1,9,17,25,65,7..., dimensions={0} | all-to-all | bytes 262144 | tf_op jit(solution)/shard_map/all_to_all | solution.py:308
  110.8 0.5 solve.5
  111.3 11.7 %all_to_all.107 = f32[16,2,128]{2,1,0:T(2,128)S(1)} all-to-all(f32[16,2,128]{2,1,0:T(2,128)S(1)} %bitcast.39), channel_id=1, replica_groups={{0,1,2,3,4,5,6,7,32,33,34,35,36,37,38,39},{8,9,10,11,12,13,14,15,40,41,..., dimensions={0} | all-to-all | bytes 32768 | tf_op jit(solution)/shard_map/all_to_all | solution.py:308
  123.0 2.6 %correct.1 = (f32[8,300]{1,0:T(8,128)}, f32[1,32768]{1,0:T(1,128)}) custom-call(f32[8,32768]{1,0:T(8,128)S(1)} %bitcast.23, f32[1,32768]{1,0:T(1,128)S(1)} %copy-done.1, s32[1,32768]{1,0:T(1,128)S(1)} %copy-done.2, f32[32,128]{1,0:T(8,128)S(1)} %bitcast.40), custom_call_target="tpu_custom_call" | custom-call | tf_op jit(solution)/shard_map/correct/pallas_call | solution.py:292
  (3 shorter events, 0.1 us)
Async XLA Ops:
  0.6 48.4 %copy-start = (f32[1,8,32768]{2,1,0:T(8,128)S(1)}, f32[1,8,32768]{2,1,0:T(8,128)}, u32[]{:S(2)}) copy-start(f32[1,8,32768]{2,1,0:T(8,128)} %param.5) | copy-start | bytes 3145732
  23.4 25.7 %copy-start.2 = (s32[1,32768]{1,0:T(1,128)S(1)}, s32[1,32768]{1,0:T(1,128)}, u32[]{:S(2)}) copy-start(s32[1,32768]{1,0:T(1,128)} %chan_ref.1) | copy-start | bytes 393220
  36.8 12.3 %copy-start.1 = (f32[1,32768]{1,0:T(1,128)S(1)}, f32[1,32768]{1,0:T(1,128)}, u32[]{:S(2)}) copy-start(f32[1,32768]{1,0:T(1,128)} %dep_ref.1) | copy-start | bytes 393220
  37.3 11.8 %copy-start.4 = (s32[1,300]{1,0:T(1,128)S(1)}, s32[1,300]{1,0:T(1,128)}, u32[]{:S(2)}) copy-start(s32[1,300]{1,0:T(1,128)} %refs_4_.5) | copy-start | bytes 3604
  49.0 0.7 copy-start.3

commit v3 on v2

--- a/solution.py
+++ b/solution.py
@@ -20,6 +20,7 @@
 FEATS = 48
 WIDE = 2 * FEATS
 CHUNK = 16384
+TILE = SUB * LANES
 
 NEAR = [
     [(CORES * x + c) * YS * ZS + ZS * y + z for c in range(CORES) for z in range(ZS)]
@@ -43,8 +44,8 @@
     return jnp.take_along_axis(table, index, axis=1, mode="promise_in_bounds")
 
 
-def spread(x, i):
-    return jnp.broadcast_to(x[i : i + 1, :], (SUB, LANES))
+def spread(x, i, rows=SUB):
+    return jnp.broadcast_to(x[i : i + 1, :], (rows, LANES))
 
 
 def channel_tables(ref):
@@ -90,13 +91,27 @@
     return tables
 
 
+def gather_sums(tiles):
+    row, _ = iotas()
+    step = SUB // 2
+    while step:
+        low = (row & step) == 0
+        half = len(tiles) // 2
+        tiles = [
+            jnp.where(low, a + pltpu.roll(a, SUB - step, 0), b + pltpu.roll(b, step, 0))
+            for a, b in zip(tiles[:half], tiles[half:])
+        ]
+        step //= 2
+    return tiles[0]
+
+
 def fit(predictors, channels, tables):
-    parts = []
-    for g in range(predictors.shape[1] // LANES):
-        at = slice(g * LANES, (g + 1) * LANES)
-        index = jnp.broadcast_to(channels[:, at], (SUB, LANES))
-        parts.append(predictors[:, at] * pick(tables, index))
-    return jnp.sum(jnp.concatenate(parts, axis=1), axis=0, keepdims=True)
+    return gather_sums(
+        [
+            predictors[:, g * LANES : (g + 1) * LANES] * pick(tables, spread(channels, g))
+            for g in range(SUB)
+        ]
+    )
 
 
 def block_rows(ref):
@@ -108,10 +123,16 @@
     )
 
 
+def tile_of(ref, t):
+    return ref[t * SUB : (t + 1) * SUB, :]
+
+
 def statistics_kernel(first, *refs):
     if first:
-        *sources, out_ref, pred_ref, dep_ref, chan_ref, decay_ref, ridge_ref, sems = refs
-        targets = (pred_ref, dep_ref, chan_ref, decay_ref, ridge_ref)
+        *sources, decay_ref, ridge_ref, out_ref, pred_ref, dep_ref, chan_ref = refs[:-3]
+        decay_copy, ridge_copy, sems = refs[-3:]
+        sources = [*sources, decay_ref, ridge_ref]
+        targets = (pred_ref, dep_ref, chan_ref, decay_copy, ridge_copy)
         copies = [
             pltpu.make_async_copy(source, target, sems.at[n])
             for n, (source, target) in enumerate(zip(sources, targets))
@@ -121,36 +142,47 @@
         for copy in copies:
             copy.wait()
     else:
-        pred_ref, dep_ref, chan_ref, decay_ref, ridge_ref, got_ref, out_ref = refs
+        pred_ref, dep_ref, chan_ref, got_ref, out_ref = refs
         tables = build_tables(got_ref)
-    row_id = lax.broadcasted_iota(jnp.int32, (SPLIT, CHUNK), 0)
+    row_id = lax.broadcasted_iota(jnp.int32, (SPLIT, LANES), 0)
 
     sums = jnp.zeros((2 * WIDE, SPLIT), jnp.float32)
     for start in range(0, pred_ref.shape[1], CHUNK):
-        at = slice(start, start + CHUNK)
-        p = pred_ref[:, at]
-        d = dep_ref[:, at]
-        c = chan_ref[:, at]
-        residual = d if first else d - fit(p, c, tables)
-        weight = EDGE / jnp.maximum(jnp.abs(residual), EDGE)
-        wp = p * weight
-        rows = [wp * p]
-        for offset in range(1, 5):
-            rows.append(wp * pltpu.roll(p, SUB - offset, 0))
-        rows.append(wp * d)
-        feats = jnp.concatenate(rows, axis=0)
-        head = feats.astype(jnp.bfloat16)
-        tail = (feats - head.astype(jnp.float32)).astype(jnp.bfloat16)
-        upper = c >= SPLIT
-        in_upper = upper.astype(jnp.float32).astype(jnp.bfloat16)
-        in_lower = 1.0 - in_upper
-        columns = jnp.concatenate(
-            [head * in_lower, head * in_upper, tail * in_lower, tail * in_upper], axis=0
-        )
-        local = jnp.where(upper, c - SPLIT, c)
-        hot = (row_id == local).astype(jnp.float32).astype(jnp.bfloat16)
+        columns, hots = [], []
+        for t in range(start // TILE, (start + CHUNK) // TILE):
+            p = pred_ref[:, t * TILE : (t + 1) * TILE]
+            d = tile_of(dep_ref, t)
+            c = tile_of(chan_ref, t)
+            residual = d if first else d - fit(p, c, tables)
+            weight = EDGE / jnp.maximum(jnp.abs(residual), EDGE)
+            upper = c >= SPLIT
+            local = jnp.where(upper, c - SPLIT, c)
+            upper = upper.astype(jnp.float32)
+            for g in range(SUB):
+                pg = p[:, g * LANES : (g + 1) * LANES]
+                wp = pg * spread(weight, g)
+                rows = [wp * pg]
+                for offset in range(1, 5):
+                    rows.append(wp * pltpu.roll(pg, SUB - offset, 0))
+                rows.append(wp * spread(d, g))
+                feats = jnp.concatenate(rows, axis=0)
+                head = feats.astype(jnp.bfloat16)
+                tail = (feats - head.astype(jnp.float32)).astype(jnp.bfloat16)
+                in_upper = spread(upper, g, FEATS).astype(jnp.bfloat16)
+                in_lower = 1.0 - in_upper
+                columns.append(
+                    jnp.concatenate(
+                        [head * in_lower, head * in_upper, tail * in_lower, tail * in_upper],
+                        axis=0,
+                    )
+                )
+                hot = row_id == spread(local, g, SPLIT)
+                hots.append(hot.astype(jnp.float32).astype(jnp.bfloat16))
         sums = sums + lax.dot_general(
-            columns, hot, (((1,), (1,)), ((), ())), preferred_element_type=jnp.float32
+            jnp.concatenate(columns, axis=1),
+            jnp.concatenate(hots, axis=1),
+            (((1,), (1,)), ((), ())),
+            preferred_element_type=jnp.float32,
         )
 
     sums = sums[:WIDE, :] + sums[WIDE:, :]
@@ -167,8 +199,10 @@
             q, third = divmod(j, 3)
             spill = sums[(SUB + q) * BLOCKS : (SUB + q + 1) * BLOCKS, :]
             spill = pltpu.roll(spill, WIDE - 32 * third, 1)
+        elif first:
+            spill = block_rows(decay_copy if j == 6 else ridge_copy)
         else:
-            spill = block_rows(decay_ref if j == 6 else ridge_ref)
+            spill = 0.0
         rows = jnp.where(lane < WIDE, sums[j * BLOCKS : (j + 1) * BLOCKS, :], spill)
         out_ref[pl.ds(j, BLOCKS, stride=SUB), :] = rows
 
@@ -194,7 +228,8 @@
             out_ref[at : at + SUB, :] = tile
 
 
-def solve_kernel(all_ref, out_ref):
+def solve_kernel(*refs):
+    all_ref, side_ref, out_ref = refs[0], refs[-2], refs[-1]
     here = lax.axis_index("win") // CORES
     row, lane = iotas()
 
@@ -209,10 +244,12 @@
     side = [carried, carried]
     for x in range(XS):
         for i in range(CORES):
-            tile = add_tiles(all_ref, [((x * YS + y) * CORES + i) * SUB for y in range(YS)])
-            carried = take(spread(tile, 6), WIDE + slot) * carried + tile
+            starts = [((x * YS + y) * CORES + i) * SUB for y in range(YS)]
+            tile = add_tiles(all_ref, starts)
+            extra = side_ref[starts[0] : starts[0] + SUB, :]
+            carried = take(spread(extra, 6), WIDE + slot) * carried + tile
             kept[i] = jnp.where(here == x, carried, kept[i])
-            side[i] = jnp.where(here == x, tile, side[i])
+            side[i] = jnp.where(here == x, extra, side[i])
 
     tiles = []
     for i in range(CORES):
@@ -281,12 +318,12 @@
         stop = min((t + 1) * LANES, count)
         coef_ref[:, t * LANES : stop] = tables[t][:, : stop - t * LANES]
 
-    for start in range(0, pred_ref.shape[1], CHUNK):
-        at = slice(start, start + CHUNK)
-        out_ref[:, at] = dep_ref[:, at] - fit(pred_ref[:, at], chan_ref[:, at], tables)
-
-
-def call(kernel, name, out_shape, operands, scratch=(), space=pltpu.VMEM, limit=32):
+    for t in range(pred_ref.shape[1] // TILE):
+        fitted = fit(pred_ref[:, t * TILE : (t + 1) * TILE], tile_of(chan_ref, t), tables)
+        out_ref[t * SUB : (t + 1) * SUB, :] = tile_of(dep_ref, t) - fitted
+
+
+def call(kernel, name, out_shape, operands, scratch=(), space=pltpu.VMEM):
     vmem = pl.BlockSpec(memory_space=pltpu.VMEM)
     several = isinstance(out_shape, list)
     return pl.pallas_call(
@@ -296,7 +333,7 @@
         in_specs=[pl.BlockSpec(memory_space=space)] * len(operands),
         out_specs=[vmem] * len(out_shape) if several else vmem,
         scratch_shapes=list(scratch),
-        compiler_params=pltpu.CompilerParams(vmem_limit_bytes=limit << 20),
+        compiler_params=pltpu.CompilerParams(vmem_limit_bytes=32 << 20),
     )(*operands)
 
 
@@ -310,33 +347,49 @@
     )
 
 
+def first_statistics(observed, decay_rate, ridge_counts):
+    operands = [*observed, decay_rate, ridge_counts]
+    scratch = [pltpu.VMEM(x.shape, x.dtype) for x in operands[3:]]
+    scratch.append(pltpu.SemaphoreType.DMA((len(operands),)))
+    parts, *fetched = call(
+        functools.partial(statistics_kernel, True),
+        "statistics",
+        [shape(BLOCKS * SUB, LANES)] + [jax.ShapeDtypeStruct(x.shape, x.dtype) for x in observed],
+        [pltpu.with_memory_space_constraint(x, pltpu.HBM) for x in operands],
+        scratch,
+        pltpu.HBM,
+    )
+    return parts, fetched
+
+
 def body(predictors, departures, channel, decay_rate, ridge_counts):
-    observed = [predictors[0], departures, channel]
-    operands = [*observed, decay_rate, ridge_counts]
     total = departures.shape[1]
-    out = shape(BLOCKS * SUB, LANES)
-    got = None
-    for _ in range(ROUNDS):
-        if got is None:
-            scratch = [pltpu.VMEM(x.shape, x.dtype) for x in operands]
-            scratch.append(pltpu.SemaphoreType.DMA((len(operands),)))
-            kernel = functools.partial(statistics_kernel, True)
-            parts = call(kernel, "statistics", out, operands, scratch, pl.ANY, 62)
-        else:
-            kernel = functools.partial(statistics_kernel, False)
-            parts = call(kernel, "statistics", out, [*operands, got])
+    dense = (total // LANES, LANES)
+    observed = [predictors[0], departures.reshape(dense), channel.reshape(dense)]
+    parts, observed = first_statistics(observed, decay_rate, ridge_counts)
+    side = []
+    for index in range(ROUNDS):
+        if index:
+            parts = call(
+                functools.partial(statistics_kernel, False),
+                "statistics",
+                shape(BLOCKS * SUB, LANES),
+                [*observed, got],
+            )
         parts = exchange(parts, NEAR)
         pair = call(reduce_kernel, "reduce", shape(XS * YS * CORES * SUB, LANES), [parts])
         tiles = exchange(pair, ACROSS)
-        flat = call(solve_kernel, "solve", shape(2 * BLOCKS, LANES), [tiles])
+        flat = call(solve_kernel, "solve", shape(2 * BLOCKS, LANES), [tiles, *side])
+        if not index:
+            side = [tiles]
         got = exchange(flat, NEAR)
     coeffs, corrected = call(
         correct_kernel,
         "correct",
-        [shape(SUB, decay_rate.shape[1]), shape(1, total)],
+        [shape(SUB, decay_rate.shape[1]), shape(*dense)],
         [*observed, got],
     )
-    return (coeffs[None], corrected)
+    return (coeffs[None], corrected.reshape(1, total))
 
 
 def solution(mesh):

time: 126 us -> 124 us (0.984)
  no operation moved by 1% of the time
where the time goes in v3:
time: 124 us; the launch traced here: 123 us
  blocking collectives  106 us (85%)
  Pallas kernels  17.2 us (14%)
    all_to_all x9, blocking collectives, exchange(): lax.all_to_all(x, ('win', 'obs'), 0, 0, tiled=True, axis_index_groups=gro...  106 us
    pallas_call x10, Pallas kernels, call(): pl.pallas_call(kernel, name=name, out_shape=out_shape, in_specs=[pl.Block...  17.2 us

profile of v3, /device:TPU:1, one launch (start us, length us, event | category | flops | bytes accessed | tf_op | source)
XLA Modules:
  0.0 123.5 jit_solution(13622524987820631972)
XLA Ops:
  0.6 4.9 %statistics.3 = (f32[128,128]{1,0:T(8,128)S(1)}, f32[8,32768]{1,0:T(8,128)S(1)}, f32[256,128]{1,0:T(8,128)S(1)}, s32[256,128]{1,0:T(8,128)S(1)}) custom-call(f32[8,32768]{1,0:T(8,128)} %bitcast.43, f32[256,128]{1,0:T(8,128)} %bitcast.44, s32[256,128]{1,0:T(8,128)} %bitcast.45, f32[1,300]{1,0:T(1,128)} %refs_3_.1, s32[1,300]{1,0:T(1,128)} %refs_4_.1), custom_call_target="tpu_custom_call" | custom-call | tf_op jit(solution)/shard_map/statistics/pallas_call | solution.py:329
  5.5 16.9 %all_to_all.99 = f32[16,8,128]{2,1,0:T(8,128)S(1)} all-to-all(f32[16,8,128]{2,1,0:T(8,128)S(1)} %bitcast.41), channel_id=1, replica_groups={{0,1,2,3,4,5,6,7,32,33,34,35,36,37,38,39},{8,9,10,11,12,13,14,15,40,41,..., dimensions={0} | all-to-all | bytes 131072 | tf_op jit(solution)/shard_map/all_to_all | solution.py:345
  22.5 13.2 %all_to_all.100 = f32[16,16,128]{2,1,0:T(8,128)S(1)} all-to-all(f32[16,16,128]{2,1,0:T(8,128)S(1)} %bitcast.27), channel_id=1, replica_groups={{0,8,16,24,64,72,80,88,128,136,144,152,192,200,208,216},{1,9,17,25,65,7..., dimensions={0} | all-to-all | bytes 262144 | tf_op jit(solution)/shard_map/all_to_all | solution.py:345
  35.7 0.5 solve.3
  36.2 11.7 %all_to_all.101 = f32[16,2,128]{2,1,0:T(2,128)S(1)} all-to-all(f32[16,2,128]{2,1,0:T(2,128)S(1)} %bitcast.40), channel_id=1, replica_groups={{0,1,2,3,4,5,6,7,32,33,34,35,36,37,38,39},{8,9,10,11,12,13,14,15,40,41,..., dimensions={0} | all-to-all | bytes 32768 | tf_op jit(solution)/shard_map/all_to_all | solution.py:345
  48.0 4.1 %statistics.4 = f32[128,128]{1,0:T(8,128)S(1)} custom-call(f32[8,32768]{1,0:T(8,128)S(1)} %get-tuple-element.8.refs_0_.pred_ref, f32[256,128]{1,0:T(8,128)S(1)} %get-tuple-element.9.refs_1_.dep_ref, s32[256,128]{1,0:T(8,128)S(1)} %get-tuple-element.10.refs_2_.chan_ref, f32[32,128]{1,0:T(8,128)S(1)} %bitcast.36), custom_call_target="tpu_custom_call" | custom-call | tf_op jit(solution)/shard_map/statistics/pallas_call | solution.py:329
  52.1 10.3 %all_to_all.102 = f32[16,8,128]{2,1,0:T(8,128)S(1)} all-to-all(f32[16,8,128]{2,1,0:T(8,128)S(1)} %bitcast.32), channel_id=1, replica_groups={{0,1,2,3,4,5,6,7,32,33,34,35,36,37,38,39},{8,9,10,11,12,13,14,15,40,41,..., dimensions={0} | all-to-all | bytes 131072 | tf_op jit(solution)/shard_map/all_to_all | solution.py:345
  62.4 9.8 %all_to_all.103 = f32[16,16,128]{2,1,0:T(8,128)S(1)} all-to-all(f32[16,16,128]{2,1,0:T(8,128)S(1)} %bitcast.28), channel_id=1, replica_groups={{0,8,16,24,64,72,80,88,128,136,144,152,192,200,208,216},{1,9,17,25,65,7..., dimensions={0} | all-to-all | bytes 262144 | tf_op jit(solution)/shard_map/all_to_all | solution.py:345
  72.2 0.5 solve.4
  72.7 11.7 %all_to_all.104 = f32[16,2,128]{2,1,0:T(2,128)S(1)} all-to-all(f32[16,2,128]{2,1,0:T(2,128)S(1)} %bitcast.39), channel_id=1, replica_groups={{0,1,2,3,4,5,6,7,32,33,34,35,36,37,38,39},{8,9,10,11,12,13,14,15,40,41,..., dimensions={0} | all-to-all | bytes 32768 | tf_op jit(solution)/shard_map/all_to_all | solution.py:345
  84.4 4.1 %statistics.5 = f32[128,128]{1,0:T(8,128)S(1)} custom-call(f32[8,32768]{1,0:T(8,128)S(1)} %get-tuple-element.8.refs_0_.pred_ref, f32[256,128]{1,0:T(8,128)S(1)} %get-tuple-element.9.refs_1_.dep_ref, s32[256,128]{1,0:T(8,128)S(1)} %get-tuple-element.10.refs_2_.chan_ref, f32[32,128]{1,0:T(8,128)S(1)} %bitcast.37), custom_call_target="tpu_custom_call" | custom-call | tf_op jit(solution)/shard_map/statistics/pallas_call | solution.py:329
  88.5 10.3 %all_to_all.105 = f32[16,8,128]{2,1,0:T(8,128)S(1)} all-to-all(f32[16,8,128]{2,1,0:T(8,128)S(1)} %bitcast.34), channel_id=1, replica_groups={{0,1,2,3,4,5,6,7,32,33,34,35,36,37,38,39},{8,9,10,11,12,13,14,15,40,41,..., dimensions={0} | all-to-all | bytes 131072 | tf_op jit(solution)/shard_map/all_to_all | solution.py:345
  98.9 9.8 %all_to_all.106 = f32[16,16,128]{2,1,0:T(8,128)S(1)} all-to-all(f32[16,16,128]{2,1,0:T(8,128)S(1)} %bitcast.30), channel_id=1, replica_groups={{0,8,16,24,64,72,80,88,128,136,144,152,192,200,208,216},{1,9,17,25,65,7..., dimensions={0} | all-to-all | bytes 262144 | tf_op jit(solution)/shard_map/all_to_all | solution.py:345
  108.7 0.5 solve.5
  109.2 11.7 %all_to_all.107 = f32[16,2,128]{2,1,0:T(2,128)S(1)} all-to-all(f32[16,2,128]{2,1,0:T(2,128)S(1)} %bitcast.38), channel_id=1, replica_groups={{0,1,2,3,4,5,6,7,32,33,34,35,36,37,38,39},{8,9,10,11,12,13,14,15,40,41,..., dimensions={0} | all-to-all | bytes 32768 | tf_op jit(solution)/shard_map/all_to_all | solution.py:345
  120.9 2.6 %correct.1 = (f32[8,300]{1,0:T(8,128)}, f32[256,128]{1,0:T(8,128)}) custom-call(f32[8,32768]{1,0:T(8,128)S(1)} %get-tuple-element.8.refs_0_.pred_ref, f32[256,128]{1,0:T(8,128)S(1)} %get-tuple-element.9.refs_1_.dep_ref, s32[256,128]{1,0:T(8,128)S(1)} %get-tuple-element.10.refs_2_.chan_ref, f32[32,128]{1,0:T(8,128)S(1)} %bitcast.42), custom_call_target="tpu_custom_call" | custom-call | tf_op jit(solution)/shard_map/correct/pallas_call | solution.py:329
  (3 shorter events, 0.1 us)

commit v4 on v3

--- a/solution.py
+++ b/solution.py
@@ -284,15 +284,23 @@
             column = jnp.where(row == (j - d) % SUB, offsets[d], column)
         columns.append(column)
 
-    right = blocks[5]
+    columns.append(blocks[5])
     inverse = jnp.ones((SUB, LANES), jnp.float32)
-    for j in range(SUB):
-        inv = 1.0 / spread(columns[j], j)
-        inverse = jnp.where(row == j, inv, inverse)
+    for j in range(0, SUB, 2):
+        first, cross = spread(columns[j], j), spread(columns[j + 1], j)
+        corner = spread(columns[j + 1], j + 1)
+        inv = 1.0 / first
+        ratio = cross * inv
+        second = first * (1.0 / (first * corner - cross * cross))
+        inverse = jnp.where(row == j, inv, jnp.where(row == j + 1, second, inverse))
         factor = jnp.where(row > j, columns[j] * inv, 0.0)
-        for k in range(j + 1, SUB):
-            columns[k] = columns[k] - factor * spread(columns[k], j)
-        right = right - factor * spread(right, j)
+        columns[j + 1] = columns[j + 1] - factor * cross
+        later = jnp.where(row > j + 1, columns[j + 1] * second, 0.0)
+        for k in range(j + 2, SUB + 1):
+            upper = spread(columns[k], j)
+            lower = spread(columns[k], j + 1) - ratio * upper
+            columns[k] = columns[k] - factor * upper - later * lower
+    right = columns.pop()
     answer = right * inverse
     for j in range(SUB - 1, 0, -1):
         factor = jnp.where(row < j, columns[j] * inverse, 0.0)

time: 124 us -> 124 us (level)
  no operation moved by 1% of the time
where the time goes in v4:
time: 124 us; the launch traced here: 123 us
  blocking collectives  106 us (85%)
  Pallas kernels  17.1 us (14%)
    all_to_all x9, blocking collectives, exchange(): lax.all_to_all(x, ('win', 'obs'), 0, 0, tiled=True, axis_index_groups=gro...  106 us
    pallas_call x10, Pallas kernels, call(): pl.pallas_call(kernel, name=name, out_shape=out_shape, in_specs=[pl.Block...  17.1 us

profile of v4, /device:TPU:1, one launch (start us, length us, event | category | flops | bytes accessed | tf_op | source)
XLA Modules:
  0.0 123.4 jit_solution(12821136451278378589)
XLA Ops:
  0.6 4.9 %statistics.3 = (f32[128,128]{1,0:T(8,128)S(1)}, f32[8,32768]{1,0:T(8,128)S(1)}, f32[256,128]{1,0:T(8,128)S(1)}, s32[256,128]{1,0:T(8,128)S(1)}) custom-call(f32[8,32768]{1,0:T(8,128)} %bitcast.43, f32[256,128]{1,0:T(8,128)} %bitcast.44, s32[256,128]{1,0:T(8,128)} %bitcast.45, f32[1,300]{1,0:T(1,128)} %refs_3_.1, s32[1,300]{1,0:T(1,128)} %refs_4_.1), custom_call_target="tpu_custom_call" | custom-call | tf_op jit(solution)/shard_map/statistics/pallas_call | solution.py:337
  5.5 16.9 %all_to_all.99 = f32[16,8,128]{2,1,0:T(8,128)S(1)} all-to-all(f32[16,8,128]{2,1,0:T(8,128)S(1)} %bitcast.41), channel_id=1, replica_groups={{0,1,2,3,4,5,6,7,32,33,34,35,36,37,38,39},{8,9,10,11,12,13,14,15,40,41,..., dimensions={0} | all-to-all | bytes 131072 | tf_op jit(solution)/shard_map/all_to_all | solution.py:353
  22.5 13.2 %all_to_all.100 = f32[16,16,128]{2,1,0:T(8,128)S(1)} all-to-all(f32[16,16,128]{2,1,0:T(8,128)S(1)} %bitcast.27), channel_id=1, replica_groups={{0,8,16,24,64,72,80,88,128,136,144,152,192,200,208,216},{1,9,17,25,65,7..., dimensions={0} | all-to-all | bytes 262144 | tf_op jit(solution)/shard_map/all_to_all | solution.py:353
  35.7 0.5 solve.3
  36.2 11.7 %all_to_all.101 = f32[16,2,128]{2,1,0:T(2,128)S(1)} all-to-all(f32[16,2,128]{2,1,0:T(2,128)S(1)} %bitcast.40), channel_id=1, replica_groups={{0,1,2,3,4,5,6,7,32,33,34,35,36,37,38,39},{8,9,10,11,12,13,14,15,40,41,..., dimensions={0} | all-to-all | bytes 32768 | tf_op jit(solution)/shard_map/all_to_all | solution.py:353
  47.9 4.1 %statistics.4 = f32[128,128]{1,0:T(8,128)S(1)} custom-call(f32[8,32768]{1,0:T(8,128)S(1)} %get-tuple-element.8.refs_0_.pred_ref, f32[256,128]{1,0:T(8,128)S(1)} %get-tuple-element.9.refs_1_.dep_ref, s32[256,128]{1,0:T(8,128)S(1)} %get-tuple-element.10.refs_2_.chan_ref, f32[32,128]{1,0:T(8,128)S(1)} %bitcast.36), custom_call_target="tpu_custom_call" | custom-call | tf_op jit(solution)/shard_map/statistics/pallas_call | solution.py:337
  52.0 10.3 %all_to_all.102 = f32[16,8,128]{2,1,0:T(8,128)S(1)} all-to-all(f32[16,8,128]{2,1,0:T(8,128)S(1)} %bitcast.32), channel_id=1, replica_groups={{0,1,2,3,4,5,6,7,32,33,34,35,36,37,38,39},{8,9,10,11,12,13,14,15,40,41,..., dimensions={0} | all-to-all | bytes 131072 | tf_op jit(solution)/shard_map/all_to_all | solution.py:353
  62.4 9.8 %all_to_all.103 = f32[16,16,128]{2,1,0:T(8,128)S(1)} all-to-all(f32[16,16,128]{2,1,0:T(8,128)S(1)} %bitcast.28), channel_id=1, replica_groups={{0,8,16,24,64,72,80,88,128,136,144,152,192,200,208,216},{1,9,17,25,65,7..., dimensions={0} | all-to-all | bytes 262144 | tf_op jit(solution)/shard_map/all_to_all | solution.py:353
  72.2 0.5 solve.4
  72.7 11.7 %all_to_all.104 = f32[16,2,128]{2,1,0:T(2,128)S(1)} all-to-all(f32[16,2,128]{2,1,0:T(2,128)S(1)} %bitcast.39), channel_id=1, replica_groups={{0,1,2,3,4,5,6,7,32,33,34,35,36,37,38,39},{8,9,10,11,12,13,14,15,40,41,..., dimensions={0} | all-to-all | bytes 32768 | tf_op jit(solution)/shard_map/all_to_all | solution.py:353
  84.4 4.1 %statistics.5 = f32[128,128]{1,0:T(8,128)S(1)} custom-call(f32[8,32768]{1,0:T(8,128)S(1)} %get-tuple-element.8.refs_0_.pred_ref, f32[256,128]{1,0:T(8,128)S(1)} %get-tuple-element.9.refs_1_.dep_ref, s32[256,128]{1,0:T(8,128)S(1)} %get-tuple-element.10.refs_2_.chan_ref, f32[32,128]{1,0:T(8,128)S(1)} %bitcast.37), custom_call_target="tpu_custom_call" | custom-call | tf_op jit(solution)/shard_map/statistics/pallas_call | solution.py:337
  88.5 10.3 %all_to_all.105 = f32[16,8,128]{2,1,0:T(8,128)S(1)} all-to-all(f32[16,8,128]{2,1,0:T(8,128)S(1)} %bitcast.34), channel_id=1, replica_groups={{0,1,2,3,4,5,6,7,32,33,34,35,36,37,38,39},{8,9,10,11,12,13,14,15,40,41,..., dimensions={0} | all-to-all | bytes 131072 | tf_op jit(solution)/shard_map/all_to_all | solution.py:353
  98.8 9.8 %all_to_all.106 = f32[16,16,128]{2,1,0:T(8,128)S(1)} all-to-all(f32[16,16,128]{2,1,0:T(8,128)S(1)} %bitcast.30), channel_id=1, replica_groups={{0,8,16,24,64,72,80,88,128,136,144,152,192,200,208,216},{1,9,17,25,65,7..., dimensions={0} | all-to-all | bytes 262144 | tf_op jit(solution)/shard_map/all_to_all | solution.py:353
  108.6 0.5 solve.5
  109.1 11.7 %all_to_all.107 = f32[16,2,128]{2,1,0:T(2,128)S(1)} all-to-all(f32[16,2,128]{2,1,0:T(2,128)S(1)} %bitcast.38), channel_id=1, replica_groups={{0,1,2,3,4,5,6,7,32,33,34,35,36,37,38,39},{8,9,10,11,12,13,14,15,40,41,..., dimensions={0} | all-to-all | bytes 32768 | tf_op jit(solution)/shard_map/all_to_all | solution.py:353
  120.8 2.6 %correct.1 = (f32[8,300]{1,0:T(8,128)}, f32[256,128]{1,0:T(8,128)}) custom-call(f32[8,32768]{1,0:T(8,128)S(1)} %get-tuple-element.8.refs_0_.pred_ref, f32[256,128]{1,0:T(8,128)S(1)} %get-tuple-element.9.refs_1_.dep_ref, s32[256,128]{1,0:T(8,128)S(1)} %get-tuple-element.10.refs_2_.chan_ref, f32[32,128]{1,0:T(8,128)S(1)} %bitcast.42), custom_call_target="tpu_custom_call" | custom-call | tf_op jit(solution)/shard_map/correct/pallas_call | solution.py:337
  (3 shorter events, 0.1 us)

commit v5 on v4

--- a/solution.py
+++ b/solution.py
@@ -22,15 +22,20 @@
 CHUNK = 16384
 TILE = SUB * LANES
 
+def device(x, core, y, high, low):
+    return (CORES * x + core) * YS * ZS + ZS * y + 2 * high + low
+
+
 NEAR = [
-    [(CORES * x + c) * YS * ZS + ZS * y + z for c in range(CORES) for z in range(ZS)]
+    [device(x, c, y, high, low) for c in range(CORES) for y in range(YS) for low in range(2)]
     for x in range(XS)
-    for y in range(YS)
+    for high in range(4)
 ]
 ACROSS = [
-    [(CORES * x + c) * YS * ZS + ZS * y + z for x in range(XS) for y in range(YS)]
+    [device(x, c, y, high, low) for x in range(XS) for high in range(4)]
     for c in range(CORES)
-    for z in range(ZS)
+    for y in range(YS)
+    for low in range(2)
 ]
 
 

time: 124 us -> 124 us (level)
  no operation moved by 1% of the time
where the time goes in v5:
time: 124 us; the launch traced here: 123 us
  blocking collectives  105 us (85%)
  Pallas kernels  17.1 us (14%)
    all_to_all x9, blocking collectives, exchange(): lax.all_to_all(x, ('win', 'obs'), 0, 0, tiled=True, axis_index_groups=gro...  105 us
    pallas_call x10, Pallas kernels, call(): pl.pallas_call(kernel, name=name, out_shape=out_shape, in_specs=[pl.Block...  17.1 us

profile of v5, /device:TPU:1, one launch (start us, length us, event | category | flops | bytes accessed | tf_op | source)
XLA Modules:
  0.0 123.3 jit_solution(16879425872568774869)
XLA Ops:
  0.6 4.9 %statistics.3 = (f32[128,128]{1,0:T(8,128)S(1)}, f32[8,32768]{1,0:T(8,128)S(1)}, f32[256,128]{1,0:T(8,128)S(1)}, s32[256,128]{1,0:T(8,128)S(1)}) custom-call(f32[8,32768]{1,0:T(8,128)} %bitcast.43, f32[256,128]{1,0:T(8,128)} %bitcast.44, s32[256,128]{1,0:T(8,128)} %bitcast.45, f32[1,300]{1,0:T(1,128)} %refs_3_.1, s32[1,300]{1,0:T(1,128)} %refs_4_.1), custom_call_target="tpu_custom_call" | custom-call | tf_op jit(solution)/shard_map/statistics/pallas_call | solution.py:342
  5.5 12.7 %all_to_all.99 = f32[16,8,128]{2,1,0:T(8,128)S(1)} all-to-all(f32[16,8,128]{2,1,0:T(8,128)S(1)} %bitcast.41), channel_id=1, replica_groups={{0,1,8,9,16,17,24,25,32,33,40,41,48,49,56,57},{2,3,10,11,18,19,26,27,34..., dimensions={0} | all-to-all | bytes 131072 | tf_op jit(solution)/shard_map/all_to_all | solution.py:358
  18.2 19.5 %all_to_all.100 = f32[16,16,128]{2,1,0:T(8,128)S(1)} all-to-all(f32[16,16,128]{2,1,0:T(8,128)S(1)} %bitcast.27), channel_id=1, replica_groups={{0,2,4,6,64,66,68,70,128,130,132,134,192,194,196,198},{1,3,5,7,65,67,69..., dimensions={0} | all-to-all | bytes 262144 | tf_op jit(solution)/shard_map/all_to_all | solution.py:358
  37.7 0.5 solve.3
  38.2 10.2 %all_to_all.101 = f32[16,2,128]{2,1,0:T(2,128)S(1)} all-to-all(f32[16,2,128]{2,1,0:T(2,128)S(1)} %bitcast.40), channel_id=1, replica_groups={{0,1,8,9,16,17,24,25,32,33,40,41,48,49,56,57},{2,3,10,11,18,19,26,27,34..., dimensions={0} | all-to-all | bytes 32768 | tf_op jit(solution)/shard_map/all_to_all | solution.py:358
  48.4 4.1 %statistics.4 = f32[128,128]{1,0:T(8,128)S(1)} custom-call(f32[8,32768]{1,0:T(8,128)S(1)} %get-tuple-element.8.refs_0_.pred_ref, f32[256,128]{1,0:T(8,128)S(1)} %get-tuple-element.9.refs_1_.dep_ref, s32[256,128]{1,0:T(8,128)S(1)} %get-tuple-element.10.refs_2_.chan_ref, f32[32,128]{1,0:T(8,128)S(1)} %bitcast.36), custom_call_target="tpu_custom_call" | custom-call | tf_op jit(solution)/shard_map/statistics/pallas_call | solution.py:342
  52.5 8.7 %all_to_all.102 = f32[16,8,128]{2,1,0:T(8,128)S(1)} all-to-all(f32[16,8,128]{2,1,0:T(8,128)S(1)} %bitcast.32), channel_id=1, replica_groups={{0,1,8,9,16,17,24,25,32,33,40,41,48,49,56,57},{2,3,10,11,18,19,26,27,34..., dimensions={0} | all-to-all | bytes 131072 | tf_op jit(solution)/shard_map/all_to_all | solution.py:358
  61.3 12.8 %all_to_all.103 = f32[16,16,128]{2,1,0:T(8,128)S(1)} all-to-all(f32[16,16,128]{2,1,0:T(8,128)S(1)} %bitcast.28), channel_id=1, replica_groups={{0,2,4,6,64,66,68,70,128,130,132,134,192,194,196,198},{1,3,5,7,65,67,69..., dimensions={0} | all-to-all | bytes 262144 | tf_op jit(solution)/shard_map/all_to_all | solution.py:358
  74.0 0.5 solve.4
  74.5 9.8 %all_to_all.104 = f32[16,2,128]{2,1,0:T(2,128)S(1)} all-to-all(f32[16,2,128]{2,1,0:T(2,128)S(1)} %bitcast.39), channel_id=1, replica_groups={{0,1,8,9,16,17,24,25,32,33,40,41,48,49,56,57},{2,3,10,11,18,19,26,27,34..., dimensions={0} | all-to-all | bytes 32768 | tf_op jit(solution)/shard_map/all_to_all | solution.py:358
  84.3 4.1 %statistics.5 = f32[128,128]{1,0:T(8,128)S(1)} custom-call(f32[8,32768]{1,0:T(8,128)S(1)} %get-tuple-element.8.refs_0_.pred_ref, f32[256,128]{1,0:T(8,128)S(1)} %get-tuple-element.9.refs_1_.dep_ref, s32[256,128]{1,0:T(8,128)S(1)} %get-tuple-element.10.refs_2_.chan_ref, f32[32,128]{1,0:T(8,128)S(1)} %bitcast.37), custom_call_target="tpu_custom_call" | custom-call | tf_op jit(solution)/shard_map/statistics/pallas_call | solution.py:342
  88.4 8.7 %all_to_all.105 = f32[16,8,128]{2,1,0:T(8,128)S(1)} all-to-all(f32[16,8,128]{2,1,0:T(8,128)S(1)} %bitcast.34), channel_id=1, replica_groups={{0,1,8,9,16,17,24,25,32,33,40,41,48,49,56,57},{2,3,10,11,18,19,26,27,34..., dimensions={0} | all-to-all | bytes 131072 | tf_op jit(solution)/shard_map/all_to_all | solution.py:358
  97.2 12.8 %all_to_all.106 = f32[16,16,128]{2,1,0:T(8,128)S(1)} all-to-all(f32[16,16,128]{2,1,0:T(8,128)S(1)} %bitcast.30), channel_id=1, replica_groups={{0,2,4,6,64,66,68,70,128,130,132,134,192,194,196,198},{1,3,5,7,65,67,69..., dimensions={0} | all-to-all | bytes 262144 | tf_op jit(solution)/shard_map/all_to_all | solution.py:358
  110.0 0.5 solve.5
  110.5 10.2 %all_to_all.107 = f32[16,2,128]{2,1,0:T(2,128)S(1)} all-to-all(f32[16,2,128]{2,1,0:T(2,128)S(1)} %bitcast.38), channel_id=1, replica_groups={{0,1,8,9,16,17,24,25,32,33,40,41,48,49,56,57},{2,3,10,11,18,19,26,27,34..., dimensions={0} | all-to-all | bytes 32768 | tf_op jit(solution)/shard_map/all_to_all | solution.py:358
  120.7 2.6 %correct.1 = (f32[8,300]{1,0:T(8,128)}, f32[256,128]{1,0:T(8,128)}) custom-call(f32[8,32768]{1,0:T(8,128)S(1)} %get-tuple-element.8.refs_0_.pred_ref, f32[256,128]{1,0:T(8,128)S(1)} %get-tuple-element.9.refs_1_.dep_ref, s32[256,128]{1,0:T(8,128)S(1)} %get-tuple-element.10.refs_2_.chan_ref, f32[32,128]{1,0:T(8,128)S(1)} %bitcast.42), custom_call_target="tpu_custom_call" | custom-call | tf_op jit(solution)/shard_map/correct/pallas_call | solution.py:342
  (3 shorter events, 0.1 us)
